TPU v7x, 32 devices: a whole 2x2x4 slice. The times are simulated.
32 devices in a mesh: groups: 2 (over x), seq: 16 (over z, y, core).
Axes of the slice: x: 2, y: 2, z: 4, core: 2. Of those that a mesh axis runs over, the one named last changes fastest.
Arguments:
- tokens: bfloat16 [262144, 2048], P(('groups', 'seq')), parts along dimension 0, may hold values from -6 to 6
- right_blocks: bfloat16 [256, 512, 512], P('seq'), may hold values from -0.25 to 0.25
- left_blocks: bfloat16 [512, 256, 256], P('seq'), may hold values from -0.375 to 0.375
- chan_first: bfloat16 [32, 64, 64], replicated, may hold values from -0.75 to 0.75
- chan_second: bfloat16 [64, 32, 32], replicated, may hold values from -1 to 1
Outputs:
- mixed: bfloat16 [262144, 2048], P(('groups', 'seq')), parts along dimension 0
There are 2 independent parts, one for each index of `groups`. A program takes and returns all parts, laid end to end along the dimension named above; an argument that names none is the same for every part. Nothing has to cross between parts.
All inputs are finite; a program needn't handle non-finite values.
Results may differ from a plain program's by a relative error of at most 0.007.
Values may be sent and summed in bfloat16 or wider, within the bound.
A program may use at most 384 MiB of HBM per device.

v0:
```python
import jax
import jax.numpy as jnp
from jax import lax
from jax.sharding import PartitionSpec as P


def on_device(tokens, right_blocks, left_blocks, chan_first, chan_second):
    rows_a = right_blocks.shape[0]
    block_len = right_blocks.shape[1]
    width = tokens.shape[1]
    count_k = chan_first.shape[0]
    count_m = chan_first.shape[1]
    x = tokens.reshape(rows_a, block_len, width)
    first = jnp.einsum("aob,abc->aoc", right_blocks, x, preferred_element_type=jnp.float32).astype(
        jnp.bfloat16
    )
    turned = jnp.einsum(
        "bxa,abc->xbc",
        left_blocks,
        lax.all_to_all(first, "seq", split_axis=1, concat_axis=0, tiled=True),
        preferred_element_type=jnp.float32,
    ).astype(jnp.bfloat16)
    back = lax.all_to_all(turned, "seq", split_axis=0, concat_axis=1, tiled=True)
    hidden = back.reshape(rows_a * block_len, width)
    gated = (tokens.astype(jnp.float32) * hidden.astype(jnp.float32)).astype(jnp.bfloat16)
    grouped = gated.reshape(rows_a * block_len, count_k, count_m)
    chan_mid = jnp.einsum(
        "kom,skm->sko", chan_first, grouped, preferred_element_type=jnp.float32
    ).astype(jnp.bfloat16)
    result = jnp.einsum("mok,skm->som", chan_second, chan_mid, preferred_element_type=jnp.float32)
    return result.reshape(rows_a * block_len, width).astype(jnp.bfloat16)


def solution(mesh):
    return jax.shard_map(
        on_device,
        mesh=mesh,
        in_specs=(P(("groups", "seq"), None), P("seq", None, None), P("seq", None, None), P(), P()),
        out_specs=P(("groups", "seq"), None),
        check_vma=False,
    )
```

profile of v0, /device:TPU:15, one launch (start us, length us, event | category | flops | bytes accessed | tf_op | source)
XLA Modules:
  0.0 1969.9 jit_solution(11058670894132006757)
XLA Ops:
  0.0 0.0 copy-start
  0.0 32.4 %convolution_convert_fusion.1 = bf16[16,512,2048]{2,1,0:T(8,128)(2,1)} fusion(bf16[16,512,512]{2,1,0:T(8,128)(2,1)} %param.6, bf16[16,512,2048]{2,1,0:T(8,128)(2,1)} %bitcast.29), kind=kOutput, calls=%fused_computation.10 | convolution fusion | flops 17196646400 | bytes 75497472 | tf_op jit(solution)/shard_map/aob,abc->aoc/dot_general | solution.py:14
  32.4 30.0 %copy.34 = bf16[16,512,2048]{2,0,1:T(8,128)(2,1)} copy(bf16[16,512,2048]{2,1,0:T(8,128)(2,1)} %convolution_convert_fusion.1) | data formatting | bytes 67108864 | tf_op jit(solution)/shard_map/convert_element_type | solution.py:14
  62.5 729.7 %all_to_all.27 = bf16[16,512,2048]{2,0,1:T(8,128)(2,1)} all-to-all(bf16[16,512,2048]{2,0,1:T(8,128)(2,1)} %copy.34), channel_id=1, replica_groups=mesh['groups'=2,'seq'=16] {'seq'}, dimensions={1} | all-to-all | bytes 67108864 | tf_op jit(solution)/shard_map/all_to_all | solution.py:20
  792.2 29.9 %copy.36 = bf16[16,16,32,2048]{3,2,1,0:T(8,128)(2,1)} copy(bf16[16,16,32,2048]{3,1,2,0:T(8,128)(2,1)} %bitcast.27) | data formatting | bytes 67108864 | tf_op jit(solution)/shard_map/all_to_all | solution.py:20
  822.1 54.8 %convert_bitcast_fusion.2 = bf16[256,32,2048]{0,2,1:T(8,128)(2,1)} fusion(bf16[32,256,256]{2,1,0:T(8,128)(2,1)} %param.7, bf16[256,32,2048]{2,1,0:T(8,128)(2,1)} %bitcast.26), kind=kOutput, calls=%fused_computation.8 | convolution fusion | flops 8606711808 | bytes 71303168 | tf_op jit(solution)/shard_map/bxa,abc->xbc/dot_general | solution.py:17
  876.9 47.1 %copy.38 = bf16[256,32,2048]{2,1,0:T(8,128)(2,1)} copy(bf16[256,32,2048]{0,2,1:T(8,128)(2,1)} %convert_bitcast_fusion.2) | data formatting | bytes 67108864 | tf_op jit(solution)/shard_map/convert_element_type | solution.py:22
  924.1 0.0 copy-start.1
  924.1 5.9 all-to-all-start.1
  930.0 0.0 copy-done.1
  930.0 0.8 copy.42
  930.8 721.3 %all-to-all-done.1 = bf16[256,32,2048]{2,1,0:T(8,128)(2,1)} async-done(((bf16[256,32,2048]{2,1,0:T(8,128)(2,1)}), bf16[256,32,2048]{2,1,0:T(8,128)(2,1)}, u32[]{:S(2)}, u32[]{:S(2)}) %all-to-all-start.1) | async-done | bytes 33554464 | tf_op jit(solution)/shard_map/all_to_all | solution.py:23
  1652.1 32.4 %convert_bitcast_fusion = f32[16,16,32,2048]{3,2,0,1:T(8,128)} fusion(bf16[16,16,32,2048]{3,2,1,0:T(8,128)(2,1)} %bitcast.12), kind=kLoop, calls=%fused_computation | loop fusion | flops 16777216 | bytes 100663296 | tf_op jit(solution)/shard_map/convert_element_type | solution.py:25
  1684.6 43.8 %copy.39 = f32[16,16,32,2048]{3,2,1,0:T(8,128)} copy(f32[16,16,32,2048]{3,2,0,1:T(8,128)} %convert_bitcast_fusion) | data formatting | bytes 134217728 | tf_op jit(solution)/shard_map/convert_element_type | solution.py:25
  1728.4 42.5 %fusion = bf16[8192,2048]{1,0:T(8,128)(2,1)} fusion(f32[16,16,32,2048]{3,2,1,0:T(8,128)} %copy.39, bf16[8192,2048]{1,0:T(8,128)(2,1)} %param.5), kind=kLoop, calls=%fused_computation.2 | loop fusion | flops 50331648 | bytes 134217728 | tf_op jit(solution)/shard_map/convert_element_type | solution.py:25
  1770.9 40.6 %copy.40 = bf16[8192,2048]{0,1:T(8,128)(2,1)} copy(bf16[8192,2048]{1,0:T(8,128)(2,1)} %fusion) | data formatting | bytes 67108864 | tf_op jit(solution)/shard_map/convert_element_type | solution.py:25
  1811.5 0.0 copy-done
  1811.5 23.3 %convolution_convert_fusion = bf16[32,8192,64]{1,2,0:T(8,128)(2,1)} fusion(bf16[32,64,64]{2,1,0:T(8,128)(2,1)S(1)} %copy-done, bf16[8192,32,64]{0,2,1:T(8,128)(2,1)} %bitcast.25), kind=kOutput, calls=%fused_computation.9 | convolution fusion | flops 2164260864 | bytes 67371008 | tf_op jit(solution)/shard_map/kom,skm->sko/dot_general | solution.py:27
  1834.8 61.5 %convert_bitcast_fusion.1 = bf16[8192,32,64]{0,1,2:T(8,128)(2,1)} fusion(bf16[64,32,32]{2,1,0:T(8,128)(2,1)S(1)} %copy.42, bf16[32,8192,64]{1,2,0:T(8,128)(2,1)} %convolution_convert_fusion), kind=kOutput, calls=%fused_computation.7 | convolution fusion | flops 1090519040 | bytes 67239936 | tf_op jit(solution)/shard_map/mok,skm->som/dot_general | solution.py:30
  1896.3 29.4 %copy.43 = bf16[8192,32,64]{0,2,1:T(8,128)(2,1)} copy(bf16[8192,32,64]{0,1,2:T(8,128)(2,1)} %convert_bitcast_fusion.1) | data formatting | bytes 67108864 | tf_op jit(solution)/shard_map/convert_element_type | solution.py:31
  1925.7 44.2 %copy.44 = bf16[8192,2048]{1,0:T(8,128)(2,1)} copy(bf16[8192,2048]{0,1:T(8,128)(2,1)} %bitcast.28) | data formatting | bytes 67108864 | tf_op jit(solution)/shard_map/convert_element_type | solution.py:31
Async XLA Ops:
  0.0 1811.5 %copy-start = (bf16[32,64,64]{2,1,0:T(8,128)(2,1)S(1)}, bf16[32,64,64]{2,1,0:T(8,128)(2,1)}, u32[]{:S(2)}) copy-start(bf16[32,64,64]{2,1,0:T(8,128)(2,1)} %param.8) | copy-start | bytes 786436
  924.1 6.0 copy-start.1
  924.1 728.1 %all-to-all-start.1 = ((bf16[256,32,2048]{2,1,0:T(8,128)(2,1)}), bf16[256,32,2048]{2,1,0:T(8,128)(2,1)}, u32[]{:S(2)}, u32[]{:S(2)}) async-start(bf16[256,32,2048]{2,1,0:T(8,128)(2,1)} %copy.38), calls=%async_computation.1 | async-start | bytes 67108864 | tf_op jit(solution)/shard_map/all_to_all | solution.py:23
where the time goes:
time: 1970 us
  blocking collectives  730 us (37%)
  waiting for transfers between devices  721 us (37%)
  local copies, waits for them, and re-layouts  266 us (14%)
  matrix products  172 us (9%)
  other arithmetic  75 us (4%)
    all_to_all x1, blocking collectives, on_device(): lax.all_to_all(first, 'seq', split_axis=1, concat_axis=0, tiled=True)  730 us
    all_to_all x1, waiting for transfers between devices, on_device(): lax.all_to_all(turned, 'seq', split_axis=0, concat_axis=1, tiled=True)  721 us
    convert_element_type x2, local copies, waits for them, and re-layouts, on_device(): return result.reshape(rows_a * block_len, width).astype(jnp.bfloat16)  73.6 us
    dot_general x1, matrix products, on_device(): jnp.einsum('mok,skm->som', chan_second, chan_mid, preferred_element_type=...  61.5 us
    dot_general x1, matrix products, on_device(): jnp.einsum('bxa,abc->xbc', left_blocks, lax.all_to_all(first, 'seq', spli...  54.8 us
    convert_element_type x1, local copies, waits for them, and re-layouts, on_device(): turned = jnp.einsum('bxa,abc->xbc', left_blocks, lax.all_to_all(first, 's...  47.1 us
    convert_element_type x1, local copies, waits for them, and re-layouts, on_device(): hidden.astype(jnp.float32)  43.8 us
    convert_element_type x1, other arithmetic, on_device(): (tokens.astype(jnp.float32) * hidden.astype(jnp.float32)).astype(jnp.bflo...  42.5 us
  transfers between devices with their start and end apart: 1, of which 1 were waited for; matrix products, arithmetic and copies ran while one was open for 0% of the time, Pallas kernels for 0%

commit v1 on v0

--- a/solution.py
+++ b/solution.py
@@ -2,6 +2,31 @@
 import jax.numpy as jnp
 from jax import lax
 from jax.sharding import PartitionSpec as P
+
+
+def cards_use(row_data, mesh_name, array_dim, where_dim=1):
+    outcome_arr = lax.axis_size(mesh_name)
+    z1 = lax.axis_index(mesh_name)
+    right_arr, inter = (outcome_arr, z1)
+    part_next = row_data.shape[array_dim] // right_arr
+    f_now = list(row_data.shape)
+    f_now[array_dim] = part_next
+    k_now = f_now[where_dim]
+    f_now[where_dim] = k_now * right_arr
+    shaped = jnp.zeros(f_now, row_data.dtype)
+    for i0 in range(right_arr):
+        mat_out = lax.dynamic_slice_in_dim(
+            row_data, (inter ^ i0) * part_next, part_next, axis=array_dim
+        )
+        if i0:
+            trail = []
+            for dev_j in range(right_arr):
+                trail.append((dev_j, dev_j ^ i0))
+            mat_out = lax.ppermute(mat_out, mesh_name, trail)
+        shaped = lax.dynamic_update_slice_in_dim(
+            shaped, mat_out, (inter ^ i0) * k_now, axis=where_dim
+        )
+    return shaped
 
 
 def on_device(tokens, right_blocks, left_blocks, chan_first, chan_second):
@@ -20,7 +45,7 @@
         lax.all_to_all(first, "seq", split_axis=1, concat_axis=0, tiled=True),
         preferred_element_type=jnp.float32,
     ).astype(jnp.bfloat16)
-    back = lax.all_to_all(turned, "seq", split_axis=0, concat_axis=1, tiled=True)
+    back = cards_use(turned, "seq", 0)
     hidden = back.reshape(rows_a * block_len, width)
     gated = (tokens.astype(jnp.float32) * hidden.astype(jnp.float32)).astype(jnp.bfloat16)
     grouped = gated.reshape(rows_a * block_len, count_k, count_m)

time: 1970 us -> 2350 us (1.19)
  the two profiles are of different devices: /device:TPU:15 before, /device:TPU:17 now
where the time goes in v1:
time: 2350 us; the launch traced here: 2340 us
  waiting for transfers between devices  1200 us (51%)
  local copies, waits for them, and re-layouts  717 us (31%)
  starting transfers between devices  206 us (9%)
  matrix products  142 us (6%)
  other arithmetic  75.1 us (3%)
    all_to_all x1, waiting for transfers between devices, on_device(): lax.all_to_all(first, 'seq', split_axis=1, concat_axis=0, tiled=True)  721 us
    ppermute x15, waiting for transfers between devices, cards_use(): mat_out = lax.ppermute(mat_out, mesh_name, trail)  480 us
    dynamic_update_slice x17, local copies, waits for them, and re-layouts, cards_use(): lax.dynamic_update_slice_in_dim(shaped, mat_out, (inter ^ i0) * k_now, ax...  425 us
    ppermute x15, starting transfers between devices, cards_use(): mat_out = lax.ppermute(mat_out, mesh_name, trail)  199 us
    unnamed x35, local copies, waits for them, and re-layouts  116 us
    convert_element_type x2, local copies, waits for them, and re-layouts, on_device(): return result.reshape(rows_a * block_len, width).astype(jnp.bfloat16)  73.6 us
    dot_general x1, matrix products, on_device(): jnp.einsum('mok,skm->som', chan_second, chan_mid, preferred_element_type=...  61.8 us
  transfers between devices with their start and end apart: 16, of which 11 were waited for; matrix products, arithmetic and copies ran while one was open for 6% of the time, Pallas kernels for 0%

profile of v1, /device:TPU:17, one launch (start us, length us, event | category | flops | bytes accessed | tf_op | source)
XLA Modules:
  0.0 2342.1 jit_solution(17707304306989541762)
XLA Ops:
  0.0 32.4 %convolution_convert_fusion.1 = bf16[16,512,2048]{2,1,0:T(8,128)(2,1)} fusion(bf16[16,512,512]{2,1,0:T(8,128)(2,1)} %param.6, bf16[16,512,2048]{2,1,0:T(8,128)(2,1)} %bitcast.55), kind=kOutput, calls=%fused_computation.5 | convolution fusion | flops 17196646400 | bytes 75497472 | tf_op jit(solution)/shard_map/aob,abc->aoc/dot_general | solution.py:39
  32.4 30.0 %copy.18 = bf16[16,512,2048]{2,0,1:T(8,128)(2,1)} copy(bf16[16,512,2048]{2,1,0:T(8,128)(2,1)} %convolution_convert_fusion.1) | data formatting | bytes 67108864 | tf_op jit(solution)/shard_map/convert_element_type | solution.py:39
  62.5 7.1 all-to-all-start
  69.7 721.1 %all-to-all-done = bf16[16,512,2048]{2,0,1:T(8,128)(2,1)} async-done(((bf16[16,512,2048]{2,0,1:T(8,128)(2,1)}), bf16[16,512,2048]{2,0,1:T(8,128)(2,1)}, u32[]{:S(2)}, u32[]{:S(2)}) %all-to-all-start) | async-done | bytes 33554464 | tf_op jit(solution)/shard_map/all_to_all | solution.py:45
  790.8 22.9 copy.19
  813.7 24.5 %convolution_convert_fusion.2 = bf16[32,2048,256]{1,2,0:T(8,128)(2,1)} fusion(bf16[32,256,256]{2,1,0:T(8,128)(2,1)} %param.7, bf16[256,32,2048]{2,0,1:T(8,128)(2,1)} %bitcast.53), kind=kOutput, calls=%fused_computation.6 | convolution fusion | flops 8606711808 | bytes 71303168 | tf_op jit(solution)/shard_map/bxa,abc->xbc/dot_general | solution.py:42
  838.2 20.7 dynamic-slice_bitcast_fusion
  858.9 0.9 collective-permute-start
  859.8 0.0 collective-permute-start.1
  859.8 1.7 collective-permute-start.2
  861.5 0.0 collective-permute-start.3
  861.5 1.8 collective-permute-start.4
  863.3 0.5 collective-permute-done
  863.8 0.9 collective-permute-start.5
  864.7 42.5 %collective-permute-done.1 = bf16[16,32,2048]{2,0,1:T(8,128)(2,1)S(1)} collective-permute-done((bf16[16,32,2048]{2,0,1:T(8,128)(2,1)}, bf16[16,32,2048]{2,0,1:T(8,128)(2,1)S(1)}, u32[]{:S(2)}, u32[]{:S(2)}) %collective-permute-start.1) | collective-permute-done | bytes 2097184 | tf_op jit(solution)/shard_map/ppermute | solution.py:25
  907.2 2.2 collective-permute-start.6
  909.4 43.2 %collective-permute-done.2 = bf16[16,32,2048]{2,0,1:T(8,128)(2,1)S(1)} collective-permute-done((bf16[16,32,2048]{2,0,1:T(8,128)(2,1)S(1)}, bf16[16,32,2048]{2,0,1:T(8,128)(2,1)S(1)}, u32[]{:S(2)}, u32[]{:S(2)}) %collective-permute-start.2) | collective-permute-done | bytes 2097184 | tf_op jit(solution)/shard_map/ppermute | solution.py:25
  952.6 0.0 collective-permute-start.7
  952.6 0.0 collective-permute-done.3
  952.6 2.5 collective-permute-start.8
  955.1 1.3 copy-done.6
  956.5 0.3 collective-permute-start.9
  956.7 40.8 %copy.17 = bf16[8192,2048]{0,1:T(8,128)(2,1)} copy(bf16[8192,2048]{1,0:T(8,128)(2,1)} %param.5) | data formatting | bytes 67108864 | tf_op args[0]
  997.5 1.5 copy.23
  999.1 16.0 broadcast_in_dim.3
  1015.1 3.2 bitcast_dynamic-update-slice_fusion
  1018.3 1.5 constant_dynamic-update-slice_fusion.13
  1019.8 3.2 constant_dynamic-update-slice_fusion.12
  1022.9 62.3 %collective-permute-done.5 = bf16[16,32,2048]{2,0,1:T(8,128)(2,1)} collective-permute-done((bf16[16,32,2048]{2,0,1:T(8,128)(2,1)}, bf16[16,32,2048]{2,0,1:T(8,128)(2,1)}, u32[]{:S(2)}, u32[]{:S(2)}) %collective-permute-start.5) | collective-permute-done | bytes 2097184 | tf_op jit(solution)/shard_map/ppermute | solution.py:25
  1085.3 4.6 collective-permute-start.10
  1089.8 1.5 constant_dynamic-update-slice_fusion.11
  1091.3 38.9 %collective-permute-done.6 = bf16[16,32,2048]{2,0,1:T(8,128)(2,1)} collective-permute-done((bf16[16,32,2048]{2,0,1:T(8,128)(2,1)}, bf16[16,32,2048]{2,0,1:T(8,128)(2,1)}, u32[]{:S(2)}, u32[]{:S(2)}) %collective-permute-start.6) | collective-permute-done | bytes 2097184 | tf_op jit(solution)/shard_map/ppermute | solution.py:25
  1130.2 0.5 collective-permute-start.11
  1130.7 1.5 constant_dynamic-update-slice_fusion.10
  1132.2 1.8 collective-permute-start.12
  1134.0 1.5 constant_dynamic-update-slice_fusion.9
  1135.4 0.0 collective-permute-done.8
  1135.4 179.4 %collective-permute-start.13 = (bf16[16,32,2048]{2,0,1:T(8,128)(2,1)S(1)}, bf16[16,32,2048]{2,0,1:T(8,128)(2,1)S(1)}, u32[]{:S(2)}, u32[]{:S(2)}) collective-permute-start(bf16[16,32,2048]{2,0,1:T(8,128)(2,1)S(1)} %copy-done.2), channel_id=1, source_target_pairs={{0,14},{1,15},{2,12},{3,13},{4,10},{5,11},{6,8},{7,9},{8,6},{9,7},... | collective-permute-start | bytes 6291464 | tf_op jit(solution)/shard_map/ppermute | solution.py:25
  1314.8 3.2 constant_dynamic-update-slice_fusion.8
  1318.0 84.8 %collective-permute-done.9 = bf16[16,32,2048]{2,0,1:T(8,128)(2,1)} collective-permute-done((bf16[16,32,2048]{2,0,1:T(8,128)(2,1)}, bf16[16,32,2048]{2,0,1:T(8,128)(2,1)}, u32[]{:S(2)}, u32[]{:S(2)}) %collective-permute-start.9) | collective-permute-done | bytes 2097184 | tf_op jit(solution)/shard_map/ppermute | solution.py:25
  1402.8 2.4 collective-permute-start.14
  1405.2 3.2 constant_dynamic-update-slice_fusion.7
  1408.4 3.2 constant_dynamic-update-slice_fusion.6
  1411.5 3.2 constant_dynamic-update-slice_fusion.5
  1414.7 3.2 constant_dynamic-update-slice_fusion.4
  1417.9 74.7 %collective-permute-done.10 = bf16[16,32,2048]{2,0,1:T(8,128)(2,1)S(1)} collective-permute-done((bf16[16,32,2048]{2,0,1:T(8,128)(2,1)S(1)}, bf16[16,32,2048]{2,0,1:T(8,128)(2,1)S(1)}, u32[]{:S(2)}, u32[]{:S(2)}) %collective-permute-start.10) | collective-permute-done | bytes 2097184 | tf_op jit(solution)/shard_map/ppermute | solution.py:25
  1492.6 1.5 constant_dynamic-update-slice_fusion.3
  1494.0 44.7 %collective-permute-done.11 = bf16[16,32,2048]{2,0,1:T(8,128)(2,1)S(1)} collective-permute-done((bf16[16,32,2048]{2,0,1:T(8,128)(2,1)S(1)}, bf16[16,32,2048]{2,0,1:T(8,128)(2,1)S(1)}, u32[]{:S(2)}, u32[]{:S(2)}) %collective-permute-start.11) | collective-permute-done | bytes 2097184 | tf_op jit(solution)/shard_map/ppermute | solution.py:25
  1538.7 1.5 constant_dynamic-update-slice_fusion.2
  1540.2 43.9 %collective-permute-done.12 = bf16[16,32,2048]{2,0,1:T(8,128)(2,1)S(1)} collective-permute-done((bf16[16,32,2048]{2,0,1:T(8,128)(2,1)S(1)}, bf16[16,32,2048]{2,0,1:T(8,128)(2,1)S(1)}, u32[]{:S(2)}, u32[]{:S(2)}) %collective-permute-start.12) | collective-permute-done | bytes 2097184 | tf_op jit(solution)/shard_map/ppermute | solution.py:25
  1584.1 1.5 constant_dynamic-update-slice_fusion.1
  1585.6 44.5 %collective-permute-done.13 = bf16[16,32,2048]{2,0,1:T(8,128)(2,1)S(1)} collective-permute-done((bf16[16,32,2048]{2,0,1:T(8,128)(2,1)S(1)}, bf16[16,32,2048]{2,0,1:T(8,128)(2,1)S(1)}, u32[]{:S(2)}, u32[]{:S(2)}) %collective-permute-start.13) | collective-permute-done | bytes 2097184 | tf_op jit(solution)/shard_map/ppermute | solution.py:25
  1630.0 1.5 constant_dynamic-update-slice_fusion
  1631.5 49.9 %copy.20 = bf16[16,512,2048]{1,0,2:T(8,128)(2,1)} copy(bf16[16,512,2048]{2,0,1:T(8,128)(2,1)} %constant_dynamic-update-slice_fusion) | data formatting | bytes 67108864 | tf_op jit(solution)/shard_map/dynamic_update_slice | solution.py:26
  1681.4 0.0 collective-permute-done.14
  1681.4 12.8 copy.21
  1694.2 341.4 %dynamic_update_slice.63 = bf16[16,512,2048]{1,0,2:T(8,128)(2,1)} dynamic-update-slice(bf16[16,512,2048]{1,0,2:T(8,128)(2,1)} %copy.20, bf16[16,32,2048]{1,0,2:T(8,128)(2,1)} %copy.21, s32[]{:T(128)} %constant.1.clone.1, s32[]{:T(128)S(6)} %select_n.127, s32[]{:T(128)} %constant.1.clone.1) | dynamic-update-slice | bytes 4194308 | tf_op jit(solution)/shard_map/dynamic_update_slice | solution.py:26
  2035.6 32.4 %convert_element_type.42 = f32[16,512,2048]{1,0,2:T(8,128)} convert(bf16[16,512,2048]{1,0,2:T(8,128)(2,1)} %dynamic_update_slice.63) | non-fusion elementwise | flops 16777216 | bytes 100663296 | tf_op jit(solution)/shard_map/convert_element_type | solution.py:50
  2068.0 72.6 %copy.26 = f32[256,8,16,512]{3,1,2,0:T(8,128)} copy(f32[256,8,16,512]{3,2,1,0:T(8,128)} %bitcast.25) | data formatting | bytes 134217728
  2140.6 42.7 %multiply_convert_fusion = bf16[8192,2048]{0,1:T(8,128)(2,1)} fusion(f32[8192,2048]{0,1:T(8,128)} %bitcast.27, bf16[8192,2048]{0,1:T(8,128)(2,1)} %copy.17), kind=kLoop, calls=%fused_computation | loop fusion | flops 50331648 | bytes 134217728 | tf_op jit(solution)/shard_map/convert_element_type | solution.py:50
  2183.3 23.0 convolution_convert_fusion
  2206.3 61.8 %convert_bitcast_fusion = bf16[8192,32,64]{0,1,2:T(8,128)(2,1)} fusion(bf16[64,32,32]{2,1,0:T(8,128)(2,1)S(1)} %copy-done.1, bf16[32,8192,64]{1,2,0:T(8,128)(2,1)} %convolution_convert_fusion), kind=kOutput, calls=%fused_computation.3 | convolution fusion | flops 1090519040 | bytes 67239936 | tf_op jit(solution)/shard_map/mok,skm->som/dot_general | solution.py:55
  2268.2 29.4 %copy.24 = bf16[8192,32,64]{0,2,1:T(8,128)(2,1)} copy(bf16[8192,32,64]{0,1,2:T(8,128)(2,1)} %convert_bitcast_fusion) | data formatting | bytes 67108864 | tf_op jit(solution)/shard_map/convert_element_type | solution.py:56
  2297.6 44.2 %copy.25 = bf16[8192,2048]{1,0:T(8,128)(2,1)} copy(bf16[8192,2048]{0,1:T(8,128)(2,1)} %bitcast.54) | data formatting | bytes 67108864 | tf_op jit(solution)/shard_map/convert_element_type | solution.py:56
  (33 shorter events, 0.1 us)
Async XLA Ops:
  0.0 2183.3 %copy-start = (bf16[32,64,64]{2,1,0:T(8,128)(2,1)S(1)}, bf16[32,64,64]{2,1,0:T(8,128)(2,1)}, u32[]{:S(2)}) copy-start(bf16[32,64,64]{2,1,0:T(8,128)(2,1)} %param.8) | copy-start | bytes 786436
  62.5 728.3 %all-to-all-start = ((bf16[16,512,2048]{2,0,1:T(8,128)(2,1)}), bf16[16,512,2048]{2,0,1:T(8,128)(2,1)}, u32[]{:S(2)}, u32[]{:S(2)}) async-start(bf16[16,512,2048]{2,0,1:T(8,128)(2,1)} %copy.18), calls=%async_computation | async-start | bytes 67108864 | tf_op jit(solution)/shard_map/all_to_all | solution.py:45
  858.9 4.9 collective-permute-start
  859.8 47.4 %collective-permute-start.1 = (bf16[16,32,2048]{2,0,1:T(8,128)(2,1)}, bf16[16,32,2048]{2,0,1:T(8,128)(2,1)S(1)}, u32[]{:S(2)}, u32[]{:S(2)}) collective-permute-start(bf16[16,32,2048]{2,0,1:T(8,128)(2,1)} %get-tuple-element.18), channel_id=1, source_target_pairs={{0,2},{1,3},{2,0},{3,1},{4,6},{5,7},{6,4},{7,5},{8,10},{9,11},{10,... | collective-permute-start | bytes 6291464 | tf_op jit(solution)/shard_map/ppermute | solution.py:25
  859.8 92.8 %collective-permute-start.2 = (bf16[16,32,2048]{2,0,1:T(8,128)(2,1)S(1)}, bf16[16,32,2048]{2,0,1:T(8,128)(2,1)S(1)}, u32[]{:S(2)}, u32[]{:S(2)}) collective-permute-start(bf16[16,32,2048]{2,0,1:T(8,128)(2,1)S(1)} %get-tuple-element.17), channel_id=1, source_target_pairs={{0,3},{1,2},{2,1},{3,0},{4,7},{5,6},{6,5},{7,4},{8,11},{9,10},{10,... | collective-permute-start | bytes 6291464 | tf_op jit(solution)/shard_map/ppermute | solution.py:25
  861.5 91.1 %collective-permute-start.3 = (bf16[16,32,2048]{2,0,1:T(8,128)(2,1)S(1)}, bf16[16,32,2048]{2,0,1:T(8,128)(2,1)S(1)}, u32[]{:S(2)}, u32[]{:S(2)}) collective-permute-start(bf16[16,32,2048]{2,0,1:T(8,128)(2,1)S(1)} %get-tuple-element.16), channel_id=1, source_target_pairs={{0,4},{1,5},{2,6},{3,7},{4,0},{5,1},{6,2},{7,3},{8,12},{9,13},{10,... | collective-permute-start | bytes 6291464 | tf_op jit(solution)/shard_map/ppermute | solution.py:25
  861.5 93.6 %collective-permute-start.4 = (bf16[16,32,2048]{2,0,1:T(8,128)(2,1)S(1)}, bf16[16,32,2048]{2,0,1:T(8,128)(2,1)S(1)}, u32[]{:S(2)}, u32[]{:S(2)}) collective-permute-start(bf16[16,32,2048]{2,0,1:T(8,128)(2,1)S(1)} %get-tuple-element.15), channel_id=1, source_target_pairs={{0,5},{1,4},{2,7},{3,6},{4,1},{5,0},{6,3},{7,2},{8,13},{9,12},{10,... | collective-permute-start | bytes 6291464 | tf_op jit(solution)/shard_map/ppermute | solution.py:25
  863.8 92.6 %copy-start.12 = (bf16[16,32,2048]{2,0,1:T(8,128)(2,1)}, bf16[16,32,2048]{2,0,1:T(8,128)(2,1)S(1)}, u32[]{:S(2)}) copy-start(bf16[16,32,2048]{2,0,1:T(8,128)(2,1)S(1)} %collective-permute-done) | copy-start | bytes 6291460
  863.8 221.4 %collective-permute-start.5 = (bf16[16,32,2048]{2,0,1:T(8,128)(2,1)}, bf16[16,32,2048]{2,0,1:T(8,128)(2,1)}, u32[]{:S(2)}, u32[]{:S(2)}) collective-permute-start(bf16[16,32,2048]{2,0,1:T(8,128)(2,1)} %get-tuple-element.14), channel_id=1, source_target_pairs={{0,6},{1,7},{2,4},{3,5},{4,2},{5,3},{6,0},{7,1},{8,14},{9,15},{10,... | collective-permute-start | bytes 6291464 | tf_op jit(solution)/shard_map/ppermute | solution.py:25
  907.2 49.2 %copy-start.14 = (bf16[16,32,2048]{2,0,1:T(8,128)(2,1)}, bf16[16,32,2048]{2,0,1:T(8,128)(2,1)S(1)}, u32[]{:S(2)}) copy-start(bf16[16,32,2048]{2,0,1:T(8,128)(2,1)S(1)} %collective-permute-done.1) | copy-start | bytes 6291460
  907.2 223.0 %collective-permute-start.6 = (bf16[16,32,2048]{2,0,1:T(8,128)(2,1)}, bf16[16,32,2048]{2,0,1:T(8,128)(2,1)}, u32[]{:S(2)}, u32[]{:S(2)}) collective-permute-start(bf16[16,32,2048]{2,0,1:T(8,128)(2,1)} %get-tuple-element.13), channel_id=1, source_target_pairs={{0,7},{1,6},{2,5},{3,4},{4,3},{5,2},{6,1},{7,0},{8,15},{9,14},{10,... | collective-permute-start | bytes 6291464 | tf_op jit(solution)/shard_map/ppermute | solution.py:25
  952.6 3.8 copy-start.10
  952.6 179.6 %collective-permute-start.7 = (bf16[16,32,2048]{2,0,1:T(8,128)(2,1)}, bf16[16,32,2048]{2,0,1:T(8,128)(2,1)}, u32[]{:S(2)}, u32[]{:S(2)}) collective-permute-start(bf16[16,32,2048]{2,0,1:T(8,128)(2,1)} %get-tuple-element.12), channel_id=1, source_target_pairs={{0,8},{1,9},{2,10},{3,11},{4,12},{5,13},{6,14},{7,15},{8,0},{9,1},... | collective-permute-start | bytes 6291464 | tf_op jit(solution)/shard_map/ppermute | solution.py:25
  952.6 3.8 copy-start.8
  952.6 182.8 %collective-permute-start.8 = (bf16[16,32,2048]{2,0,1:T(8,128)(2,1)}, bf16[16,32,2048]{2,0,1:T(8,128)(2,1)}, u32[]{:S(2)}, u32[]{:S(2)}) collective-permute-start(bf16[16,32,2048]{2,0,1:T(8,128)(2,1)} %get-tuple-element.11), channel_id=1, source_target_pairs={{0,9},{1,8},{2,11},{3,10},{4,13},{5,12},{6,15},{7,14},{8,1},{9,0},... | collective-permute-start | bytes 6291464 | tf_op jit(solution)/shard_map/ppermute | solution.py:25
  955.1 1.3 copy-start.6
  956.5 446.3 %collective-permute-start.9 = (bf16[16,32,2048]{2,0,1:T(8,128)(2,1)}, bf16[16,32,2048]{2,0,1:T(8,128)(2,1)}, u32[]{:S(2)}, u32[]{:S(2)}) collective-permute-start(bf16[16,32,2048]{2,0,1:T(8,128)(2,1)} %get-tuple-element.10), channel_id=1, source_target_pairs={{0,10},{1,11},{2,8},{3,9},{4,14},{5,15},{6,12},{7,13},{8,2},{9,3},... | collective-permute-start | bytes 6291464 | tf_op jit(solution)/shard_map/ppermute | solution.py:25
  956.7 40.8 %copy-start.15 = (bf16[64,32,32]{0,2,1:T(8,128)(2,1)S(1)}, bf16[64,32,32]{0,2,1:T(8,128)(2,1)}, u32[]{:S(2)}) copy-start(bf16[64,32,32]{0,2,1:T(8,128)(2,1)} %param.9) | copy-start | bytes 393220
  999.1 19.2 copy-start.13
  999.1 86.2 %copy-start.5 = (bf16[16,32,2048]{2,0,1:T(8,128)(2,1)S(1)}, bf16[16,32,2048]{2,0,1:T(8,128)(2,1)}, u32[]{:S(2)}) copy-start(bf16[16,32,2048]{2,0,1:T(8,128)(2,1)} %get-tuple-element.9) | copy-start | bytes 6291460
  999.1 90.8 %copy-start.11 = (bf16[16,32,2048]{2,0,1:T(8,128)(2,1)S(1)}, bf16[16,32,2048]{2,0,1:T(8,128)(2,1)}, u32[]{:S(2)}) copy-start(bf16[16,32,2048]{2,0,1:T(8,128)(2,1)} %copy-done.10) | copy-start | bytes 6291460
  999.1 131.1 %copy-start.4 = (bf16[16,32,2048]{2,0,1:T(8,128)(2,1)S(1)}, bf16[16,32,2048]{2,0,1:T(8,128)(2,1)}, u32[]{:S(2)}) copy-start(bf16[16,32,2048]{2,0,1:T(8,128)(2,1)} %get-tuple-element.8) | copy-start | bytes 6291460
  999.1 131.6 %copy-start.9 = (bf16[16,32,2048]{2,0,1:T(8,128)(2,1)S(1)}, bf16[16,32,2048]{2,0,1:T(8,128)(2,1)}, u32[]{:S(2)}) copy-start(bf16[16,32,2048]{2,0,1:T(8,128)(2,1)} %copy-done.8) | copy-start | bytes 6291460
  999.1 133.1 %copy-start.3 = (bf16[16,32,2048]{2,0,1:T(8,128)(2,1)S(1)}, bf16[16,32,2048]{2,0,1:T(8,128)(2,1)}, u32[]{:S(2)}) copy-start(bf16[16,32,2048]{2,0,1:T(8,128)(2,1)} %get-tuple-element.7) | copy-start | bytes 6291460
  999.1 134.9 %copy-start.7 = (bf16[16,32,2048]{2,0,1:T(8,128)(2,1)S(1)}, bf16[16,32,2048]{2,0,1:T(8,128)(2,1)}, u32[]{:S(2)}) copy-start(bf16[16,32,2048]{2,0,1:T(8,128)(2,1)} %copy-done.6) | copy-start | bytes 6291460
  999.1 136.3 %copy-start.2 = (bf16[16,32,2048]{2,0,1:T(8,128)(2,1)S(1)}, bf16[16,32,2048]{2,0,1:T(8,128)(2,1)}, u32[]{:S(2)}) copy-start(bf16[16,32,2048]{2,0,1:T(8,128)(2,1)} %get-tuple-element.6) | copy-start | bytes 6291460
  1085.3 407.3 %collective-permute-start.10 = (bf16[16,32,2048]{2,0,1:T(8,128)(2,1)S(1)}, bf16[16,32,2048]{2,0,1:T(8,128)(2,1)S(1)}, u32[]{:S(2)}, u32[]{:S(2)}) collective-permute-start(bf16[16,32,2048]{2,0,1:T(8,128)(2,1)S(1)} %copy-done.5), channel_id=1, source_target_pairs={{0,11},{1,10},{2,9},{3,8},{4,15},{5,14},{6,13},{7,12},{8,3},{9,2},... | collective-permute-start | bytes 6291464 | tf_op jit(solution)/shard_map/ppermute | solution.py:25
  1130.2 408.5 %collective-permute-start.11 = (bf16[16,32,2048]{2,0,1:T(8,128)(2,1)S(1)}, bf16[16,32,2048]{2,0,1:T(8,128)(2,1)S(1)}, u32[]{:S(2)}, u32[]{:S(2)}) collective-permute-start(bf16[16,32,2048]{2,0,1:T(8,128)(2,1)S(1)} %copy-done.4), channel_id=1, source_target_pairs={{0,12},{1,13},{2,14},{3,15},{4,8},{5,9},{6,10},{7,11},{8,4},{9,5},... | collective-permute-start | bytes 6291464 | tf_op jit(solution)/shard_map/ppermute | solution.py:25
  1132.2 451.9 %collective-permute-start.12 = (bf16[16,32,2048]{2,0,1:T(8,128)(2,1)S(1)}, bf16[16,32,2048]{2,0,1:T(8,128)(2,1)S(1)}, u32[]{:S(2)}, u32[]{:S(2)}) collective-permute-start(bf16[16,32,2048]{2,0,1:T(8,128)(2,1)S(1)} %copy-done.3), channel_id=1, source_target_pairs={{0,13},{1,12},{2,15},{3,14},{4,9},{5,8},{6,11},{7,10},{8,5},{9,4},... | collective-permute-start | bytes 6291464 | tf_op jit(solution)/shard_map/ppermute | solution.py:25
  1135.4 494.6 %collective-permute-start.13 = (bf16[16,32,2048]{2,0,1:T(8,128)(2,1)S(1)}, bf16[16,32,2048]{2,0,1:T(8,128)(2,1)S(1)}, u32[]{:S(2)}, u32[]{:S(2)}) collective-permute-start(bf16[16,32,2048]{2,0,1:T(8,128)(2,1)S(1)} %copy-done.2), channel_id=1, source_target_pairs={{0,14},{1,15},{2,12},{3,13},{4,10},{5,11},{6,8},{7,9},{8,6},{9,7},... | collective-permute-start | bytes 6291464 | tf_op jit(solution)/shard_map/ppermute | solution.py:25
  1402.8 278.6 %collective-permute-start.14 = (bf16[16,32,2048]{2,0,1:T(8,128)(2,1)S(1)}, bf16[16,32,2048]{2,0,1:T(8,128)(2,1)}, u32[]{:S(2)}, u32[]{:S(2)}) collective-permute-start(bf16[16,32,2048]{2,0,1:T(8,128)(2,1)S(1)} %get-tuple-element.5), channel_id=1, source_target_pairs={{0,15},{1,14},{2,13},{3,12},{4,11},{5,10},{6,9},{7,8},{8,7},{9,6},... | collective-permute-start | bytes 6291464 | tf_op jit(solution)/shard_map/ppermute | solution.py:25
  2183.3 23.0 copy-start.1
